TPU v7x, 32 devices: a whole 2x2x4 slice. The times are simulated.
32 devices in a mesh: center: 8 (over z, y), rep: 4 (over x, core).
Axes of the slice: x: 2, y: 2, z: 4, core: 2. Of those that a mesh axis runs over, the one named last changes fastest.
Arguments:
- faces: bfloat16 [2048, 512], P(('center', 'rep')), may hold values from -1800 to 1800
- w_first: bfloat16 [512, 512], replicated, may hold values from -1.1 to 1.1
- w_second: bfloat16 [512, 512], replicated, may hold values from -1.1 to 1.1
- gain_first: float32 [512], replicated, may hold values from 0.46 to 1.54
- bias_first: float32 [512], replicated, may hold values from -3 to 3
- gain_second: float32 [512], replicated, may hold values from 0.46 to 1.54
- centers: float32 [16384, 512], P('center'), may hold values from -6 to 6
- momentum: float32 [16384, 512], P('center'), may hold values from -1.2 to 1.2
- sample_index: int32 [1024], P('center'), may hold values from 0 to 2047, as said below
- live_count: int32 [8], P('center'), may hold values from 16 to 128, as said below
- labels: int32 [2048], P(('center', 'rep')), may hold values from 0 to 1023, as said below
Outputs:
- loss: float32 [2048], P(('center', 'rep'))
- feat_grad: float32 [2048, 512], P(('center', 'rep'))
- new_centers: float32 [1024, 512], P('center')
- new_momentum: float32 [1024, 512], P('center')
Inputs may be any that keep to these rules, and one draw needn't show every extreme that they name: `sample_index`: the 128 entries of one shard are distinct rows of that shard. The live slots of a shard are its first live_count entries; some shard has 128 of them and some shard 128 // 8. `labels`: each label is a live sampled slot, counted over all shards' lists in shard order.
All inputs are finite; a program needn't handle non-finite values.
Results may differ from a plain program's by a relative error of at most 0.0075.
Values may be sent and summed in bfloat16 or wider, within the bound.
No kernel may reach another device: no remote copies, remote signals or barrier semaphores. Data moves between devices by JAX's collectives and lax.ppermute only.
A program may use at most 64 MiB of HBM per device.

v0:
```python
import jax
import jax.numpy as jnp
from jax import lax
from jax.sharding import PartitionSpec as P

LOGIT_SCALE = 64.0
COS_MARGIN = 0.35
LEARN_RATE = 0.5
MOMENT_COEF = 0.9
DECAY_COEF = 0.0005
NORM_EPS = 1e-05
LENGTH_EPS = 1e-06


def batch_norm(values, gain_vec, sample_count):
    summed, squares = lax.psum((jnp.sum(values, 0), jnp.sum(values * values, 0)), "rep")
    mean_vec = summed / sample_count
    spread = squares / sample_count - mean_vec * mean_vec
    return gain_vec * (values - mean_vec) * lax.rsqrt(spread + NORM_EPS)


def momentum_step(raw_grad, picked, center_len, center_unit, picked_momentum, live_slot):
    center_radial = jnp.sum(center_unit * raw_grad, 1, keepdims=True)
    center_grad = (raw_grad - center_unit * center_radial) / center_len
    velocity = MOMENT_COEF * picked_momentum + center_grad + DECAY_COEF * picked
    velocity = jnp.where(live_slot[:, None], velocity, picked_momentum)
    placed = jnp.where(live_slot[:, None], picked - LEARN_RATE * velocity, picked)
    return (placed, velocity)


def per_device(
    faces,
    w_first,
    w_second,
    gain_first,
    bias_first,
    gain_second,
    centers,
    momentum,
    sample_index,
    live_count,
    labels,
):
    face_rows = faces.shape[0]
    width = faces.shape[1]
    sample_count = face_rows * lax.axis_size("rep")
    first_out = jnp.dot(faces, w_first, preferred_element_type=jnp.float32)
    hidden = jnp.maximum(batch_norm(first_out, gain_first, sample_count) + bias_first, 0.0).astype(
        jnp.bfloat16
    )
    second = jnp.dot(hidden, w_second, preferred_element_type=jnp.float32)
    feature = batch_norm(second, gain_second, sample_count)
    length = jnp.sqrt(jnp.sum(feature * feature, 1, keepdims=True) + LENGTH_EPS)
    unit_rows = feature / length
    unit_low = unit_rows.astype(jnp.bfloat16)
    all_units, all_labels = (
        lax.all_gather(unit_low, "center", axis=0, tiled=True),
        lax.all_gather(labels, "center", axis=0, tiled=True),
    )
    my_shard = lax.axis_index("center")
    picked = jnp.take(centers, sample_index, axis=0)
    picked_momentum = jnp.take(momentum, sample_index, axis=0)
    center_len = jnp.sqrt(jnp.sum(picked * picked, 1, keepdims=True) + LENGTH_EPS)
    center_unit = picked / center_len
    center_low = center_unit.astype(jnp.bfloat16)
    slot_count = picked.shape[0]
    slot_ids = jnp.arange(slot_count, dtype=jnp.int32)
    live_slot = slot_ids < live_count[0]
    first_slot = my_shard * slot_count
    group_rows = all_units.shape[0]
    block_rows = min(1024, group_rows)
    block_total_count = group_rows // block_rows
    unit_blocks = all_units.reshape(block_total_count, block_rows, width)
    mark_blocks = all_labels.reshape(block_total_count, block_rows)

    def target_of(mark_block):
        return (mark_block - first_slot)[:, None] == slot_ids[None, :]

    def partials(element):
        cosine = jnp.einsum("fd,sd->fs", element[0], center_low, preferred_element_type=jnp.float32)
        target = target_of(element[1])
        logits = LOGIT_SCALE * (cosine - COS_MARGIN * target.astype(jnp.float32))
        exponent = jnp.where(live_slot[None, :], jnp.exp(logits), 0.0)
        return (exponent, jnp.sum(exponent, 1), jnp.sum(jnp.where(target, logits, 0.0), 1))

    exponent_blocks, local_total, local_target = lax.map(partials, (unit_blocks, mark_blocks))
    softmax_total, target_logit = lax.psum(
        (local_total.reshape(group_rows), local_target.reshape(group_rows)), "center"
    )
    group_loss = jnp.log(softmax_total) - target_logit
    loss = lax.dynamic_slice_in_dim(group_loss, my_shard * face_rows, face_rows, 0)
    total_blocks = softmax_total.reshape(block_total_count, block_rows)

    def grad_weight(exponent, mark_block, block_total):
        target = target_of(mark_block)
        return (
            LOGIT_SCALE * (exponent / block_total[:, None] - target.astype(jnp.float32))
        ).astype(jnp.bfloat16)

    start_sum = jnp.zeros((slot_count, width), jnp.float32)

    def both_block(running, element):
        weight = grad_weight(element[2], element[1], element[3])
        running = running + jnp.einsum(
            "fs,fd->sd", weight, element[0], preferred_element_type=jnp.float32
        )
        return (running, jnp.dot(weight, center_low, preferred_element_type=jnp.float32))

    center_raw, unit_terms = lax.scan(
        both_block, start_sum, (unit_blocks, mark_blocks, exponent_blocks, total_blocks)
    )
    unit_grad = lax.psum_scatter(
        unit_terms.reshape(group_rows, width), "center", scatter_dimension=0, tiled=True
    )
    radial = jnp.sum(unit_rows * unit_grad, 1, keepdims=True)
    feat_grad = (unit_grad - unit_rows * radial) / length
    raw_grad = lax.psum(center_raw, "rep")
    new_centers, new_momentum = momentum_step(
        raw_grad, picked, center_len, center_unit, picked_momentum, live_slot
    )
    return (loss, feat_grad, new_centers, new_momentum)


def solution(mesh):
    return jax.shard_map(
        per_device,
        mesh=mesh,
        in_specs=(
            P(("center", "rep"), None),
            P(),
            P(),
            P(),
            P(),
            P(),
            P("center", None),
            P("center", None),
            P("center"),
            P("center"),
            P(("center", "rep")),
        ),
        out_specs=(
            P(("center", "rep")),
            P(("center", "rep"), None),
            P("center", None),
            P("center", None),
        ),
        check_vma=False,
    )
```

profile of v0, /device:TPU:0, one launch (start us, length us, event | category | flops | bytes accessed | tf_op | source)
XLA Modules:
  0.0 172.2 jit_solution(15847876268697771019)
XLA Ops:
  8.8 0.7 compare_select_fusion
  9.4 0.7 compare_and_fusion
  10.1 1.2 dynamic-slice.4
  12.0 0.9 dynamic-update-slice
  12.8 13.1 %all-reduce = s32[512]{0:T(512)S(1)} all-reduce(s32[512]{0:T(512)S(1)} %dynamic-update-slice), channel_id=1, replica_groups=mesh['center'=8,'rep'=4] {'center'}, use_global_device_ids=true, to_apply=%add | all-reduce | flops 512 | bytes 4096
  25.9 1.1 fusion.16
  27.0 5.7 %all-reduce.3 = (f32[512]{0:T(512)S(1)}, f32[512]{0:T(512)S(1)}) all-reduce(f32[512]{0:T(512)S(1)} %get-tuple-element.60, f32[512]{0:T(512)S(1)} %get-tuple-element.49), channel_id=1, replica_groups=mesh['center'=8,'rep'=4] {'rep'}, use_global_device_ids=true, to_apply=%region_3.0 | all-reduce | flops 1024 | bytes 8192 | tf_op jit(solution)/shard_map/psum | solution.py:16
  32.7 1.3 fusion.15
  34.0 6.6 %all-reduce.2 = (f32[512]{0:T(512)S(1)}, f32[512]{0:T(512)S(1)}) all-reduce(f32[512]{0:T(512)S(1)} %get-tuple-element.48, f32[512]{0:T(512)S(1)} %get-tuple-element.47), channel_id=1, replica_groups=mesh['center'=8,'rep'=4] {'rep'}, use_global_device_ids=true, to_apply=%region_7.0 | all-reduce | flops 1024 | bytes 8192 | tf_op jit(solution)/shard_map/psum | solution.py:16
  40.6 0.8 multiply_reduce_fusion.3
  41.5 0.8 fusion.13
  42.2 3.1 %gather_fusion = f32[128,512]{1,0:T(8,128)S(1)} fusion(f32[2048,512]{1,0:T(8,128)} %param.19, s32[1024]{0:T(1024)S(1)} %pad_clamp_fusion), kind=kCustom, calls=%fused_computation.clone | custom fusion | bytes 524800 | tf_op jit(solution)/shard_map/jit(_take)/gather | solution.py:61
  45.5 31.2 %all_gather.6 = bf16[512,512]{1,0:T(8,128)(2,1)S(1)} all-gather(bf16[64,512]{1,0:T(8,128)(2,1)S(1)} %fusion.13), channel_id=1, replica_groups=mesh['center'=8,'rep'=4] {'center'}, dimensions={0}, use_global_device_ids=true | all-gather | bytes 589824 | tf_op jit(solution)/shard_map/all_gather | solution.py:57
  77.1 18.9 %all-reduce.1 = (f32[512]{0:T(512)S(1)}, f32[512]{0:T(512)S(1)}) all-reduce(f32[512]{0:T(512)S(1)} %get-tuple-element.46, f32[512]{0:T(512)S(1)} %get-tuple-element.45), channel_id=1, replica_groups=mesh['center'=8,'rep'=4] {'center'}, use_global_device_ids=true, to_apply=%region_13.15 | all-reduce | flops 1024 | bytes 8192 | tf_op jit(solution)/shard_map/psum | solution.py:87
  96.0 1.0 fusion.14
  97.1 1.4 fusion.4
  98.5 3.1 %gather_fusion.1 = f32[128,512]{1,0:T(8,128)S(1)} fusion(f32[2048,512]{1,0:T(8,128)} %param.20, s32[1024]{0:T(1024)S(1)} %pad_clamp_fusion), kind=kCustom, calls=%fused_computation.1.clone | custom fusion | bytes 524800 | tf_op jit(solution)/shard_map/jit(_take)/gather | solution.py:62
  101.6 0.6 dynamic_slice.19
  102.2 23.7 %all-reduce.6.cloned.1.call-done = f32[128,512]{1,0:T(8,128)} async-done(((f32[128,512]{1,0:T(8,128)}), f32[128,512]{1,0:T(8,128)}) %all-reduce.6.cloned.1.call-update) | async-done | bytes 262160 | tf_op jit(solution)/shard_map/psum | solution.py:117
  126.0 1.1 multiply_reduce_fusion
  127.1 1.9 %subtract_select_fusion = (f32[128,512]{1,0:T(8,128)}, f32[128,512]{1,0:T(8,128)}) fusion(f32[128,512]{1,0:T(8,128)S(1)} %gather_fusion, pred[128]{0:T(512)(128)(4,1)S(1)} %get-tuple-element.86, pred[128]{0:T(512)(128)(4,1)S(1)} %get-tuple-element.87, f32[128,512]{1,0:T(8,128)} %all-reduce.6.cloned.1.call-done, f32[128]{0:T(128)S(1)} %multiply_reduce_fusion, ...), kind=kLoop, calls=%fused_computation.4 | loop fusion | flops 917504 | bytes 1312000 | tf_op jit(solution)/shard_map/jit(_where)/select_n | solution.py:27
  129.1 33.0 %reduce-scatter.2.cloned.1.call-done = f32[64,512]{1,0:T(8,128)} async-done(((f32[512,512]{1,0:T(8,128)}), f32[64,512]{1,0:T(8,128)}) %reduce-scatter.2.cloned.1.call-update) | async-done | bytes 131088 | tf_op jit(solution)/shard_map/reduce_scatter | solution.py:112
  162.0 1.1 multiply_reduce_fusion.2
  163.1 1.7 subtract_divide_fusion
  (18 shorter events, 0.7 us)
Async XLA Ops:
  8.0 17.9 %copy-start = (bf16[512,512]{1,0:T(8,128)(2,1)S(1)}, bf16[512,512]{1,0:T(8,128)(2,1)}, u32[]{:S(2)}) copy-start(bf16[512,512]{1,0:T(8,128)(2,1)} %param.14) | copy-start | bytes 1572868
  8.0 118.0 %all-reduce.6.cloned.1.call-start = ((), (), s32[]{:S(2)}) async-start(), calls=%async_computation.2 | async-start | bytes 524288 | tf_op jit(solution)/shard_map/psum | solution.py:117
  97.0 65.0 %copy-start.1 = (f32[512]{0:T(512)S(1)}, f32[512]{0:T(512)}, u32[]{:S(2)}) copy-start(f32[512]{0:T(512)} %param.18) | copy-start | bytes 6148
  97.1 65.0 %reduce-scatter.2.cloned.1.call-start = ((), (), s32[]{:S(2)}) async-start(), calls=%async_computation.1 | async-start | bytes 1179648 | tf_op jit(solution)/shard_map/reduce_scatter | solution.py:112
Sparse Core Ops, SparseCore 0:
  97.2 28.7 all-reduce.5
Sparse Core Ops, SparseCore 1:
  100.9 61.0 reduce-scatter.1
where the time goes:
time: 173 us; the launch traced here: 172 us
  blocking collectives  75.5 us (44%)
  waiting for transfers between devices  56.7 us (33%)
  between operations  16.9 us (10%)
  other arithmetic  8.98 us (5%)
  local copies, waits for them, and re-layouts  8.84 us (5%)
  matrix products  5.14 us (3%)
    reduce_scatter x1, waiting for transfers between devices, per_device(): lax.psum_scatter(unit_terms.reshape(group_rows, width), 'center', scatter...  33 us
    all_gather x1, blocking collectives, per_device(): lax.all_gather(unit_low, 'center', axis=0, tiled=True)  31.2 us
    psum x1, waiting for transfers between devices, per_device(): raw_grad = lax.psum(center_raw, 'rep')  23.7 us
    psum x1, blocking collectives, per_device(): lax.psum((local_total.reshape(group_rows), local_target.reshape(group_row...  18.9 us
    unnamed x1, blocking collectives  13.1 us
    psum x2, blocking collectives, batch_norm(): lax.psum((jnp.sum(values, 0), jnp.sum(values * values, 0)), 'rep')  12.3 us
  transfers between devices with their start and end apart: 2, of which 2 were waited for; matrix products, arithmetic and copies ran while one was open for 5% of the time, Pallas kernels for 0%

commit v1 on v0

--- a/solution.py
+++ b/solution.py
@@ -53,8 +53,38 @@
     length = jnp.sqrt(jnp.sum(feature * feature, 1, keepdims=True) + LENGTH_EPS)
     unit_rows = feature / length
     unit_low = unit_rows.astype(jnp.bfloat16)
+
+    def apply_levels_all_up(array_in, at_axis):
+        carry_out, ready, arr_next = (
+            lax.axis_size("center"),
+            lax.axis_index("center"),
+            array_in.shape[at_axis],
+        )
+        pool = tuple(((dd, (dd + 1) % carry_out) for dd in range(carry_out)))
+        heap = tuple(((dd, (dd - 1) % carry_out) for dd in range(carry_out)))
+        v_now = jnp.zeros(
+            (*array_in.shape[:at_axis], carry_out * arr_next, *array_in.shape[at_axis + 1 :]),
+            array_in.dtype,
+        )
+        v_now = lax.dynamic_update_slice_in_dim(v_now, array_in, ready * arr_next, axis=at_axis)
+        g_now = local_part = array_in
+        response = carry_out // 2
+        kk = 1
+        while kk < response + 1:
+            g_now = lax.ppermute(g_now, "center", pool)
+            v_now = lax.dynamic_update_slice_in_dim(
+                v_now, g_now, (ready - kk) % carry_out * arr_next, axis=at_axis
+            )
+            if kk < carry_out - response:
+                local_part = lax.ppermute(local_part, "center", heap)
+                v_now = lax.dynamic_update_slice_in_dim(
+                    v_now, local_part, (ready + kk) % carry_out * arr_next, axis=at_axis
+                )
+            kk = kk + 1
+        return v_now
+
     all_units, all_labels = (
-        lax.all_gather(unit_low, "center", axis=0, tiled=True),
+        apply_levels_all_up(unit_low, 0),
         lax.all_gather(labels, "center", axis=0, tiled=True),
     )
     my_shard = lax.axis_index("center")

time: 173 us -> 167 us (0.965)
  blocking collectives: 75.5 us -> 41.2 us
  starting transfers between devices: 0.08 us -> 14.5 us
  waiting for transfers between devices: 56.7 us -> 69.9 us
    all_gather x1 -> x0, blocking collectives: 31.2 us -> none  [per_device(): lax.all_gather(unit_low, 'center', axis=0, tiled=True)]
    ppermute x0 -> x7, starting transfers between devices: none -> 14.4 us  [the longest x3 12 us: apply_levels_all_up(): local_part = lax.ppermute(local_part, 'center', heap)]
    ppermute x0 -> x7, waiting for transfers between devices: none -> 11.8 us  [the longest x4 11.8 us: apply_levels_all_up(): g_now = lax.ppermute(g_now, 'center', pool)]
    unnamed x1, blocking collectives: 13.1 us -> 9.91 us
    psum x2, blocking collectives: 12.3 us -> 14.1 us  [batch_norm(): lax.psum((jnp.sum(values, 0), jnp.sum(values * values, 0)), 'rep')]
    psum x1, blocking collectives: 18.9 us -> 17.1 us  [per_device(): lax.psum((local_total.reshape(group_rows), local_target.reshape(group_row...]
  transfers between devices with their start and end apart: 2 -> 9, of which waited for: 2 -> 5; matrix products, arithmetic and copies ran while one was open for 5% -> 9% of each run, Pallas kernels for 0% -> 0%
where the time goes in v1:
time: 167 us
  waiting for transfers between devices  69.9 us (42%)
  blocking collectives  41.2 us (25%)
  between operations  17.1 us (10%)
  starting transfers between devices  14.5 us (9%)
  local copies, waits for them, and re-layouts  9.96 us (6%)
  other arithmetic  8.98 us (5%)
  matrix products  5.14 us (3%)
    reduce_scatter x1, waiting for transfers between devices, per_device(): lax.psum_scatter(unit_terms.reshape(group_rows, width), 'center', scatter...  33 us
    psum x1, waiting for transfers between devices, per_device(): raw_grad = lax.psum(center_raw, 'rep')  25 us
    psum x1, blocking collectives, per_device(): lax.psum((local_total.reshape(group_rows), local_target.reshape(group_row...  17.1 us
    psum x2, blocking collectives, batch_norm(): lax.psum((jnp.sum(values, 0), jnp.sum(values * values, 0)), 'rep')  14.1 us
    ppermute x3, starting transfers between devices, apply_levels_all_up(): local_part = lax.ppermute(local_part, 'center', heap)  12 us
    ppermute x4, waiting for transfers between devices, apply_levels_all_up(): g_now = lax.ppermute(g_now, 'center', pool)  11.8 us
    unnamed x1, blocking collectives  9.91 us
  transfers between devices with their start and end apart: 9, of which 5 were waited for; matrix products, arithmetic and copies ran while one was open for 9% of the time, Pallas kernels for 0%

profile of v1, /device:TPU:0, one launch (start us, length us, event | category | flops | bytes accessed | tf_op | source)
XLA Modules:
  0.0 166.7 jit_solution(1566686209501540471)
XLA Ops:
  9.0 1.1 fusion.16
  10.1 8.4 %all-reduce.3 = (f32[512]{0:T(512)S(1)}, f32[512]{0:T(512)S(1)}) all-reduce(f32[512]{0:T(512)S(1)} %get-tuple-element.60, f32[512]{0:T(512)S(1)} %get-tuple-element.49), channel_id=1, replica_groups=mesh['center'=8,'rep'=4] {'rep'}, use_global_device_ids=true, to_apply=%region_3.0 | all-reduce | flops 1024 | bytes 8192 | tf_op jit(solution)/shard_map/psum | solution.py:16
  18.5 1.3 fusion.15
  19.8 5.8 %all-reduce.2 = (f32[512]{0:T(512)S(1)}, f32[512]{0:T(512)S(1)}) all-reduce(f32[512]{0:T(512)S(1)} %get-tuple-element.48, f32[512]{0:T(512)S(1)} %get-tuple-element.47), channel_id=1, replica_groups=mesh['center'=8,'rep'=4] {'rep'}, use_global_device_ids=true, to_apply=%region_7.0 | all-reduce | flops 1024 | bytes 8192 | tf_op jit(solution)/shard_map/psum | solution.py:16
  27.2 1.7 %collective-permute-start = (bf16[64,512]{1,0:T(8,128)(2,1)S(1)}, bf16[64,512]{1,0:T(8,128)(2,1)S(1)}, u32[]{:S(2)}, u32[]{:S(2)}) collective-permute-start(bf16[64,512]{1,0:T(8,128)(2,1)S(1)} %get-tuple-element.80), channel_id=1, source_target_pairs={{0,4},{4,8},{8,12},{12,16},{16,20},{20,24},{24,28},{28,0},{1,5},{5... | collective-permute-start | bytes 196616 | tf_op jit(solution)/shard_map/ppermute | solution.py:74
  28.9 3.1 %collective-permute-start.1 = (bf16[64,512]{1,0:T(8,128)(2,1)S(1)}, bf16[64,512]{1,0:T(8,128)(2,1)S(1)}, u32[]{:S(2)}, u32[]{:S(2)}) collective-permute-start(bf16[64,512]{1,0:T(8,128)(2,1)S(1)} %get-tuple-element.80), channel_id=1, source_target_pairs={{0,28},{4,0},{8,4},{12,8},{16,12},{20,16},{24,20},{28,24},{1,29},{... | collective-permute-start | bytes 196616 | tf_op jit(solution)/shard_map/ppermute | solution.py:79
  34.0 1.2 dynamic-slice.3
  36.8 9.9 %all-reduce = s32[512]{0:T(512)S(1)} all-reduce(s32[512]{0:T(512)S(1)} %dynamic-update-slice), channel_id=1, replica_groups=mesh['center'=8,'rep'=4] {'center'}, use_global_device_ids=true, to_apply=%add | all-reduce | flops 512 | bytes 4096
  46.7 3.1 %gather_fusion = f32[128,512]{1,0:T(8,128)S(1)} fusion(f32[2048,512]{1,0:T(8,128)} %param.19, s32[1024]{0:T(1024)S(1)} %pad_clamp_fusion), kind=kCustom, calls=%fused_computation.clone | custom fusion | bytes 524800 | tf_op jit(solution)/shard_map/jit(_take)/gather | solution.py:91
  50.8 4.1 %collective-permute-start.3 = (bf16[64,512]{1,0:T(8,128)(2,1)S(1)}, bf16[64,512]{1,0:T(8,128)(2,1)S(1)}, u32[]{:S(2)}, u32[]{:S(2)}) collective-permute-start(bf16[64,512]{1,0:T(8,128)(2,1)S(1)} %collective-permute-done.1), channel_id=1, source_target_pairs={{0,28},{4,0},{8,4},{12,8},{16,12},{20,16},{24,20},{28,24},{1,29},{... | collective-permute-start | bytes 196616 | tf_op jit(solution)/shard_map/ppermute | solution.py:79
  54.9 2.2 %collective-permute-done.2 = bf16[64,512]{1,0:T(8,128)(2,1)S(1)} collective-permute-done((bf16[64,512]{1,0:T(8,128)(2,1)S(1)}, bf16[64,512]{1,0:T(8,128)(2,1)S(1)}, u32[]{:S(2)}, u32[]{:S(2)}) %collective-permute-start.2) | collective-permute-done | bytes 65568 | tf_op jit(solution)/shard_map/ppermute | solution.py:74
  57.1 4.8 %collective-permute-start.5 = (bf16[64,512]{1,0:T(8,128)(2,1)S(1)}, bf16[64,512]{1,0:T(8,128)(2,1)S(1)}, u32[]{:S(2)}, u32[]{:S(2)}) collective-permute-start(bf16[64,512]{1,0:T(8,128)(2,1)S(1)} %collective-permute-done.3), channel_id=1, source_target_pairs={{0,28},{4,0},{8,4},{12,8},{16,12},{20,16},{24,20},{28,24},{1,29},{... | collective-permute-start | bytes 196616 | tf_op jit(solution)/shard_map/ppermute | solution.py:79
  62.0 2.7 %collective-permute-done.4 = bf16[64,512]{1,0:T(8,128)(2,1)S(1)} collective-permute-done((bf16[64,512]{1,0:T(8,128)(2,1)S(1)}, bf16[64,512]{1,0:T(8,128)(2,1)S(1)}, u32[]{:S(2)}, u32[]{:S(2)}) %collective-permute-start.4) | collective-permute-done | bytes 65568 | tf_op jit(solution)/shard_map/ppermute | solution.py:74
  64.7 6.9 %collective-permute-done.6 = bf16[64,512]{1,0:T(8,128)(2,1)S(1)} collective-permute-done((bf16[64,512]{1,0:T(8,128)(2,1)S(1)}, bf16[64,512]{1,0:T(8,128)(2,1)S(1)}, u32[]{:S(2)}, u32[]{:S(2)}) %collective-permute-start.6) | collective-permute-done | bytes 65568 | tf_op jit(solution)/shard_map/ppermute | solution.py:74
  72.0 17.1 %all-reduce.1 = (f32[512]{0:T(512)S(1)}, f32[512]{0:T(512)S(1)}) all-reduce(f32[512]{0:T(512)S(1)} %get-tuple-element.46, f32[512]{0:T(512)S(1)} %get-tuple-element.45), channel_id=1, replica_groups=mesh['center'=8,'rep'=4] {'center'}, use_global_device_ids=true, to_apply=%region_13.15 | all-reduce | flops 1024 | bytes 8192 | tf_op jit(solution)/shard_map/psum | solution.py:117
  89.2 1.0 fusion.14
  90.2 1.4 fusion.4
  91.7 3.1 %gather_fusion.1 = f32[128,512]{1,0:T(8,128)S(1)} fusion(f32[2048,512]{1,0:T(8,128)} %param.20, s32[1024]{0:T(1024)S(1)} %pad_clamp_fusion), kind=kCustom, calls=%fused_computation.1.clone | custom fusion | bytes 524800 | tf_op jit(solution)/shard_map/jit(_take)/gather | solution.py:92
  95.4 25.0 %all-reduce.6.cloned.1.call-done = f32[128,512]{1,0:T(8,128)} async-done(((f32[128,512]{1,0:T(8,128)}), f32[128,512]{1,0:T(8,128)}) %all-reduce.6.cloned.1.call-update) | async-done | bytes 262160 | tf_op jit(solution)/shard_map/psum | solution.py:147
  120.4 1.1 multiply_reduce_fusion
  121.5 2.0 %subtract_select_fusion = (f32[128,512]{1,0:T(8,128)}, f32[128,512]{1,0:T(8,128)}) fusion(f32[128,512]{1,0:T(8,128)S(1)} %gather_fusion, pred[128]{0:T(512)(128)(4,1)S(1)} %get-tuple-element.88, pred[128]{0:T(512)(128)(4,1)S(1)} %get-tuple-element.89, f32[128,512]{1,0:T(8,128)} %all-reduce.6.cloned.1.call-done, f32[128]{0:T(128)S(1)} %multiply_reduce_fusion, ...), kind=kLoop, calls=%fused_computation.4 | loop fusion | flops 917504 | bytes 1312000 | tf_op jit(solution)/shard_map/jit(_where)/select_n | solution.py:27
  123.5 33.0 %reduce-scatter.2.cloned.1.call-done = f32[64,512]{1,0:T(8,128)} async-done(((f32[512,512]{1,0:T(8,128)}), f32[64,512]{1,0:T(8,128)}) %reduce-scatter.2.cloned.1.call-update) | async-done | bytes 131088 | tf_op jit(solution)/shard_map/reduce_scatter | solution.py:142
  156.5 1.1 multiply_reduce_fusion.2
  157.6 1.7 subtract_divide_fusion
  (39 shorter events, 6.9 us)
Async XLA Ops:
  8.0 1.0 copy-start
  8.0 112.4 %all-reduce.6.cloned.1.call-start = ((), (), s32[]{:S(2)}) async-start(), calls=%async_computation.2 | async-start | bytes 524288 | tf_op jit(solution)/shard_map/psum | solution.py:147
  27.2 22.8 %collective-permute-start = (bf16[64,512]{1,0:T(8,128)(2,1)S(1)}, bf16[64,512]{1,0:T(8,128)(2,1)S(1)}, u32[]{:S(2)}, u32[]{:S(2)}) collective-permute-start(bf16[64,512]{1,0:T(8,128)(2,1)S(1)} %get-tuple-element.80), channel_id=1, source_target_pairs={{0,4},{4,8},{8,12},{12,16},{16,20},{20,24},{24,28},{28,0},{1,5},{5... | collective-permute-start | bytes 196616 | tf_op jit(solution)/shard_map/ppermute | solution.py:74
  28.9 21.8 %collective-permute-start.1 = (bf16[64,512]{1,0:T(8,128)(2,1)S(1)}, bf16[64,512]{1,0:T(8,128)(2,1)S(1)}, u32[]{:S(2)}, u32[]{:S(2)}) collective-permute-start(bf16[64,512]{1,0:T(8,128)(2,1)S(1)} %get-tuple-element.80), channel_id=1, source_target_pairs={{0,28},{4,0},{8,4},{12,8},{16,12},{20,16},{24,20},{28,24},{1,29},{... | collective-permute-start | bytes 196616 | tf_op jit(solution)/shard_map/ppermute | solution.py:79
  50.1 7.0 %collective-permute-start.2 = (bf16[64,512]{1,0:T(8,128)(2,1)S(1)}, bf16[64,512]{1,0:T(8,128)(2,1)S(1)}, u32[]{:S(2)}, u32[]{:S(2)}) collective-permute-start(bf16[64,512]{1,0:T(8,128)(2,1)S(1)} %collective-permute-done), channel_id=1, source_target_pairs={{0,4},{4,8},{8,12},{12,16},{16,20},{20,24},{24,28},{28,0},{1,5},{5... | collective-permute-start | bytes 196616 | tf_op jit(solution)/shard_map/ppermute | solution.py:74
  50.8 6.3 %collective-permute-start.3 = (bf16[64,512]{1,0:T(8,128)(2,1)S(1)}, bf16[64,512]{1,0:T(8,128)(2,1)S(1)}, u32[]{:S(2)}, u32[]{:S(2)}) collective-permute-start(bf16[64,512]{1,0:T(8,128)(2,1)S(1)} %collective-permute-done.1), channel_id=1, source_target_pairs={{0,28},{4,0},{8,4},{12,8},{16,12},{20,16},{24,20},{28,24},{1,29},{... | collective-permute-start | bytes 196616 | tf_op jit(solution)/shard_map/ppermute | solution.py:79
  57.1 7.6 %collective-permute-start.4 = (bf16[64,512]{1,0:T(8,128)(2,1)S(1)}, bf16[64,512]{1,0:T(8,128)(2,1)S(1)}, u32[]{:S(2)}, u32[]{:S(2)}) collective-permute-start(bf16[64,512]{1,0:T(8,128)(2,1)S(1)} %collective-permute-done.2), channel_id=1, source_target_pairs={{0,4},{4,8},{8,12},{12,16},{16,20},{20,24},{24,28},{28,0},{1,5},{5... | collective-permute-start | bytes 196616 | tf_op jit(solution)/shard_map/ppermute | solution.py:74
  57.1 7.6 %collective-permute-start.5 = (bf16[64,512]{1,0:T(8,128)(2,1)S(1)}, bf16[64,512]{1,0:T(8,128)(2,1)S(1)}, u32[]{:S(2)}, u32[]{:S(2)}) collective-permute-start(bf16[64,512]{1,0:T(8,128)(2,1)S(1)} %collective-permute-done.3), channel_id=1, source_target_pairs={{0,28},{4,0},{8,4},{12,8},{16,12},{20,16},{24,20},{28,24},{1,29},{... | collective-permute-start | bytes 196616 | tf_op jit(solution)/shard_map/ppermute | solution.py:79
  64.7 7.0 %collective-permute-start.6 = (bf16[64,512]{1,0:T(8,128)(2,1)S(1)}, bf16[64,512]{1,0:T(8,128)(2,1)S(1)}, u32[]{:S(2)}, u32[]{:S(2)}) collective-permute-start(bf16[64,512]{1,0:T(8,128)(2,1)S(1)} %collective-permute-done.4), channel_id=1, source_target_pairs={{0,4},{4,8},{8,12},{12,16},{16,20},{20,24},{24,28},{28,0},{1,5},{5... | collective-permute-start | bytes 196616 | tf_op jit(solution)/shard_map/ppermute | solution.py:74
  90.2 66.3 %copy-start.1 = (f32[512]{0:T(512)S(1)}, f32[512]{0:T(512)}, u32[]{:S(2)}) copy-start(f32[512]{0:T(512)} %param.18) | copy-start | bytes 6148
  90.2 66.3 %reduce-scatter.2.cloned.1.call-start = ((), (), s32[]{:S(2)}) async-start(), calls=%async_computation.1 | async-start | bytes 1179648 | tf_op jit(solution)/shard_map/reduce_scatter | solution.py:142
Sparse Core Ops, SparseCore 0:
  90.3 30.0 all-reduce.5
Sparse Core Ops, SparseCore 1:
  94.1 62.3 reduce-scatter.1
